TPU v7x, 32 devices: a whole 2x2x4 slice. The times are simulated.
32 devices in a mesh: day: 2 (over y), stu: 16 (over z, x, core).
Axes of the slice: x: 2, y: 2, z: 4, core: 2. Of those that a mesh axis runs over, the one named last changes fastest.
Arguments:
- performance: bfloat16 [64, 128, 1024], P('day', 'stu'), may hold values from -8 to 8
- student_factor: bfloat16 [128, 256], P('stu'), may hold values from -0.5 to 0.5
- skill_factor: bfloat16 [1024, 256], replicated, may hold values from -0.1875 to 0.1875
- day_prev: float32 [64, 256], P('day'), may hold values from -6 to 6
- ar_coef: float32 [7], replicated, may hold values from -0.3 to 0.3
Outputs:
- day_factor: float32 [64, 256], P('day', 'stu')
- residual: float32 [64, 256], P('day', 'stu')
All inputs are finite; a program needn't handle non-finite values.
Results may differ from a plain program's by a relative error of at most 0.0003.
Values sent between devices are 32-bit elements; how exact they have to be, the bound alone decides.
No kernel may reach another device: no remote copies, remote signals or barrier semaphores. Data moves between devices by JAX's collectives and lax.ppermute only.
A program may use at most 64 MiB of HBM per device.

v0:
```python
import jax
import jax.numpy as jnp
from jax import lax
from jax.sharding import PartitionSpec as P

LAGS = 7
ITERS = 3
smoothing = 1.0


def shifted(block, axis, distance):
    devices = range(lax.axis_size(axis))
    route = [(i - distance, i) for i in devices if i - distance in devices]
    return lax.ppermute(block, axis, route)


def filter_rows(extended, coef, count):
    out = extended[LAGS : LAGS + count]
    for lag in range(1, LAGS + 1):
        out = out - coef[lag - 1] * extended[LAGS - lag : LAGS - lag + count]
    return out


def smooth(values, coef):
    count = values.shape[0]
    below = shifted(values[count - LAGS :], "day", 1)
    ahead_core = filter_rows(jnp.concatenate([below, values], 0), coef, count)
    above = shifted(ahead_core[:LAGS], "day", -1)
    ahead = jnp.concatenate([ahead_core, above], 0)
    out = ahead[:count]
    for lag in range(1, LAGS + 1):
        out = out - coef[lag - 1] * ahead[lag : lag + count]
    return out


def with_gram(values, gram_part):
    return jnp.dot(
        lax.all_gather(values, "stu", axis=1, tiled=True),
        gram_part,
        precision=lax.Precision.HIGHEST,
        preferred_element_type=jnp.float32,
    )


def operate(values, gram_part, coef):
    return with_gram(values, gram_part) + smoothing * smooth(values, coef)


def global_total(value):
    return lax.psum(value, ("day", "stu"))


def summed_gram(local_gram):
    return lax.psum(local_gram, "stu")


def local(performance, student_factor, skill_factor, day_prev, ar_coef):
    days, students, skills = performance.shape
    rank = skill_factor.shape[1]
    proj = jnp.dot(
        performance.reshape(days * students, skills),
        skill_factor,
        preferred_element_type=jnp.float32,
    )
    proj = proj.reshape(days, students, rank)
    local_terms = jnp.sum(proj * student_factor.astype(jnp.float32)[None], axis=1)
    local_gram = jnp.dot(student_factor.T, student_factor, preferred_element_type=jnp.float32)
    skill_gram = jnp.dot(skill_factor.T, skill_factor, preferred_element_type=jnp.float32)
    columns = rank // lax.axis_size("stu")
    first_col = lax.axis_index("stu") * columns
    gram = summed_gram(local_gram) * skill_gram
    mttkrp = lax.psum_scatter(local_terms, "stu", scatter_dimension=1, tiled=True)
    gram_part = lax.dynamic_slice_in_dim(gram, first_col, columns, 1)
    day_factor = lax.dynamic_slice_in_dim(day_prev, first_col, columns, 1)
    residual = mttkrp - operate(day_factor, gram_part, ar_coef)
    direction = residual
    norm_now = global_total(jnp.sum(residual * residual))
    for step in range(ITERS):
        image = operate(direction, gram_part, ar_coef)
        alpha = norm_now / global_total(jnp.sum(direction * image))
        day_factor = day_factor + alpha * direction
        residual = residual - alpha * image
        norm_next = global_total(jnp.sum(residual * residual))
        direction = residual + norm_next / norm_now * direction
        norm_now = norm_next
    return (day_factor, residual)


def solution(mesh):
    return jax.shard_map(
        local,
        mesh=mesh,
        in_specs=(P("day", "stu", None), P("stu", None), P(), P("day", None), P()),
        out_specs=(P("day", "stu"), P("day", "stu")),
        check_vma=False,
    )
```

profile of v0, /device:TPU:14, one launch (start us, length us, event | category | flops | bytes accessed | tf_op | source)
XLA Modules:
  0.0 491.8 jit_solution(908321572501885240)
XLA Ops:
  9.6 1.7 fusion.139
  14.3 15.5 %all_gather.12 = f32[32,256]{0,1:T(8,128)S(1)} all-gather(f32[32,16]{0,1:T(8,128)S(1)} %copy.10), channel_id=1, replica_groups=mesh['day'=2,'stu'=16] {'stu'}, dimensions={1}, use_global_device_ids=true | all-gather | bytes 34816 | tf_op jit(solution)/shard_map/all_gather | solution.py:38
  29.8 4.5 fusion.120
  34.3 4.6 collective-permute-start.1
  38.9 64.2 %all-reduce.3.cloned.1.call-done = f32[256,256]{0,1:T(8,128)} async-done(((f32[256,256]{0,1:T(8,128)}), f32[256,256]{0,1:T(8,128)}) %all-reduce.3.cloned.1.call-update) | async-done | bytes 262160 | tf_op jit(solution)/shard_map/psum | solution.py:54
  103.8 57.7 %reduce-scatter.2.cloned.1.call-done = f32[32,16]{0,1:T(8,128)} async-done(((f32[32,256]{0,1:T(8,128)}), f32[32,16]{0,1:T(8,128)}) %reduce-scatter.2.cloned.1.call-update) | async-done | bytes 2064 | tf_op jit(solution)/shard_map/reduce_scatter | solution.py:72
  161.5 5.2 %fusion.104 = f32[32,16]{0,1:T(8,128)S(1)} fusion(f32[32,16]{0,1:T(8,128)} %reduce-scatter.2.cloned.1.call-done, f32[7,16]{0,1:T(8,128)S(1)} %collective-permute-done.1, f32[32,16]{0,1:T(8,128)S(1)} %fusion.120, f32[]{:T(128)} %bitcast.7, f32[]{:T(128)} %bitcast.6, f32[]{:T(128)} %bitcast.5, f32[]{:T(128)} %bitcast.4, f32[]{:T(128)} %bitcast.3, ...), kind=kOutput, calls=%fused_computation.173 | convolution fusion | flops 1584640 | bytes 55772 | tf_op jit(solution)/shard_map/dot_general | solution.py:37
  168.1 4.2 collective-permute-done.2
  172.3 4.5 fusion.86
  178.5 15.4 %all_gather.13 = f32[32,256]{0,1:T(8,128)S(1)} all-gather(f32[32,16]{0,1:T(8,128)S(1)} %fusion.104), channel_id=1, replica_groups=mesh['day'=2,'stu'=16] {'stu'}, dimensions={1}, use_global_device_ids=true | all-gather | bytes 34816 | tf_op jit(solution)/shard_map/all_gather | solution.py:38
  193.8 5.2 %multiply_reduce_fusion.4 = (f32[]{:T(128)}, f32[]{:T(128)}, f32[32,16]{0,1:T(8,128)S(1)}) fusion(f32[32,16]{0,1:T(8,128)S(1)} %fusion.104, f32[7,16]{0,1:T(8,128)S(1)} %collective-permute-done.3, f32[32,16]{0,1:T(8,128)S(1)} %fusion.86, f32[]{:T(128)} %bitcast.7, f32[]{:T(128)} %bitcast.6, f32[]{:T(128)} %bitcast.5, f32[]{:T(128)} %bitcast.4, ...), kind=kOutput, calls=%fused_computation.235 | convolution fusion | flops 1586174 | bytes 55780 | tf_op jit(solution)/shard_map/dot_general | solution.py:37
  199.0 44.1 %all-reduce = (f32[]{:T(128)}, f32[]{:T(128)}) all-reduce(f32[]{:T(128)} %get-tuple-element.3, f32[]{:T(128)} %get-tuple-element.2), channel_id=1, replica_groups=mesh['day'=2,'stu'=16] {'day','stu'}, use_global_device_ids=true, to_apply=%region_4.0 | all-reduce | flops 2 | bytes 16 | tf_op jit(solution)/shard_map/psum | solution.py:50
  245.1 38.6 %psum.52 = f32[]{:T(128)} all-reduce(f32[]{:T(128)} %multiply_reduce_fusion.3), channel_id=1, replica_groups=mesh['day'=2,'stu'=16] {'day','stu'}, use_global_device_ids=true, to_apply=%region_8.0 | all-reduce | flops 1 | bytes 8 | tf_op jit(solution)/shard_map/psum | solution.py:50
  286.4 4.2 collective-permute-done.4
  290.7 4.5 fusion.53
  296.8 18.0 %all_gather.14 = f32[32,256]{0,1:T(8,128)S(1)} all-gather(f32[32,16]{0,1:T(8,128)S(1)} %multiply_add_fusion.2), channel_id=1, replica_groups=mesh['day'=2,'stu'=16] {'stu'}, dimensions={1}, use_global_device_ids=true | all-gather | bytes 34816 | tf_op jit(solution)/shard_map/all_gather | solution.py:38
  314.8 5.2 %multiply_reduce_fusion.2 = (f32[]{:T(128)}, f32[32,16]{0,1:T(8,128)S(1)}) fusion(f32[32,16]{0,1:T(8,128)S(1)} %multiply_add_fusion.2, f32[7,16]{0,1:T(8,128)S(1)} %collective-permute-done.5, f32[32,16]{0,1:T(8,128)S(1)} %fusion.53, f32[]{:T(128)} %bitcast.7, f32[]{:T(128)} %bitcast.6, f32[]{:T(128)} %bitcast.5, f32[]{:T(128)} %bitcast.4, f32[]{:T(128)} %bitcast.3, ...), kind=kOutput, calls=%fused_computation.231 | convolution fusion | flops 1585151 | bytes 55776 | tf_op jit(solution)/shard_map/dot_general | solution.py:37
  320.0 43.0 %psum.53 = f32[]{:T(128)} all-reduce(f32[]{:T(128)} %get-tuple-element.10), channel_id=1, replica_groups=mesh['day'=2,'stu'=16] {'day','stu'}, use_global_device_ids=true, to_apply=%region_10.0 | all-reduce | flops 1 | bytes 8 | tf_op jit(solution)/shard_map/psum | solution.py:50
  364.8 39.0 %psum.54 = f32[]{:T(128)} all-reduce(f32[]{:T(128)} %get-tuple-element.8), channel_id=1, replica_groups=mesh['day'=2,'stu'=16] {'day','stu'}, use_global_device_ids=true, to_apply=%region_12.0 | all-reduce | flops 1 | bytes 8 | tf_op jit(solution)/shard_map/psum | solution.py:50
  406.5 4.2 collective-permute-done.6
  410.8 4.5 fusion.20
  416.9 17.6 %all_gather.15 = f32[32,256]{0,1:T(8,128)S(1)} all-gather(f32[32,16]{0,1:T(8,128)S(1)} %multiply_add_fusion.1), channel_id=1, replica_groups=mesh['day'=2,'stu'=16] {'stu'}, dimensions={1}, use_global_device_ids=true | all-gather | bytes 34816 | tf_op jit(solution)/shard_map/all_gather | solution.py:38
  434.5 5.1 %multiply_reduce_fusion = (f32[]{:T(128)}, f32[32,16]{0,1:T(8,128)S(1)}) fusion(f32[32,16]{0,1:T(8,128)S(1)} %multiply_add_fusion.1, f32[7,16]{0,1:T(8,128)S(1)} %collective-permute-done.7, f32[32,16]{0,1:T(8,128)S(1)} %fusion.20, f32[]{:T(128)} %bitcast.7, f32[]{:T(128)} %bitcast.6, f32[]{:T(128)} %bitcast.5, f32[]{:T(128)} %bitcast.4, f32[]{:T(128)} %bitcast.3, ...), kind=kOutput, calls=%fused_computation.227 | convolution fusion | flops 1585151 | bytes 55776 | tf_op jit(solution)/shard_map/dot_general | solution.py:37
  439.7 43.2 %psum.55 = f32[]{:T(128)} all-reduce(f32[]{:T(128)} %get-tuple-element.6), channel_id=1, replica_groups=mesh['day'=2,'stu'=16] {'day','stu'}, use_global_device_ids=true, to_apply=%region_14.0 | all-reduce | flops 1 | bytes 8 | tf_op jit(solution)/shard_map/psum | solution.py:50
  (41 shorter events, 17.0 us)
Async XLA Ops:
  7.2 4.8 copy-start
  7.2 4.8 copy-start.1
  7.2 95.9 %all-reduce.3.cloned.1.call-start = ((), (), s32[]{:S(2)}) async-start(), calls=%async_computation.2 | async-start | bytes 524288 | tf_op jit(solution)/shard_map/psum | solution.py:54
  8.3 21.6 %collective-permute-start = (f32[7,16]{0,1:T(8,128)S(1)}, f32[7,16]{0,1:T(8,128)S(1)}, u32[]{:S(2)}, u32[]{:S(2)}) collective-permute-start(f32[7,16]{0,1:T(8,128)S(1)} %slice.333), channel_id=1, source_target_pairs={{0,16},{1,17},{2,18},{3,19},{4,20},{5,21},{6,22},{7,23},{8,24},{9,... | collective-permute-start | bytes 1352 | tf_op jit(solution)/shard_map/ppermute | solution.py:14
  11.2 0.7 copy-start.2
  11.3 150.2 %reduce-scatter.2.cloned.1.call-start = ((), (), s32[]{:S(2)}) async-start(), calls=%async_computation.1 | async-start | bytes 139264 | tf_op jit(solution)/shard_map/reduce_scatter | solution.py:72
  13.0 0.7 copy-start.3
  34.3 69.5 %collective-permute-start.1 = (f32[7,16]{0,1:T(8,128)S(1)}, f32[7,16]{0,1:T(8,128)S(1)}, u32[]{:S(2)}, u32[]{:S(2)}) collective-permute-start(f32[7,16]{0,1:T(8,128)S(1)} %bitcast.27), channel_id=1, source_target_pairs={{16,0},{17,1},{18,2},{19,3},{20,4},{21,5},{22,6},{23,7},{24,8},{25... | collective-permute-start | bytes 1352 | tf_op jit(solution)/shard_map/ppermute | solution.py:14
  166.8 5.5 %collective-permute-start.2 = (f32[7,16]{0,1:T(8,128)S(1)}, f32[7,16]{0,1:T(8,128)S(1)}, u32[]{:S(2)}, u32[]{:S(2)}) collective-permute-start(f32[7,16]{0,1:T(8,128)S(1)} %slice.359), channel_id=1, source_target_pairs={{0,16},{1,17},{2,18},{3,19},{4,20},{5,21},{6,22},{7,23},{8,24},{9,... | collective-permute-start | bytes 1352 | tf_op jit(solution)/shard_map/ppermute | solution.py:14
  176.8 17.0 %collective-permute-start.3 = (f32[7,16]{0,1:T(8,128)S(1)}, f32[7,16]{0,1:T(8,128)S(1)}, u32[]{:S(2)}, u32[]{:S(2)}) collective-permute-start(f32[7,16]{0,1:T(8,128)S(1)} %bitcast.29), channel_id=1, source_target_pairs={{16,0},{17,1},{18,2},{19,3},{20,4},{21,5},{22,6},{23,7},{24,8},{25... | collective-permute-start | bytes 1352 | tf_op jit(solution)/shard_map/ppermute | solution.py:14
  285.1 5.5 %collective-permute-start.4 = (f32[7,16]{0,1:T(8,128)S(1)}, f32[7,16]{0,1:T(8,128)S(1)}, u32[]{:S(2)}, u32[]{:S(2)}) collective-permute-start(f32[7,16]{0,1:T(8,128)S(1)} %slice.385), channel_id=1, source_target_pairs={{0,16},{1,17},{2,18},{3,19},{4,20},{5,21},{6,22},{7,23},{8,24},{9,... | collective-permute-start | bytes 1352 | tf_op jit(solution)/shard_map/ppermute | solution.py:14
  295.1 19.6 %collective-permute-start.5 = (f32[7,16]{0,1:T(8,128)S(1)}, f32[7,16]{0,1:T(8,128)S(1)}, u32[]{:S(2)}, u32[]{:S(2)}) collective-permute-start(f32[7,16]{0,1:T(8,128)S(1)} %bitcast.30), channel_id=1, source_target_pairs={{16,0},{17,1},{18,2},{19,3},{20,4},{21,5},{22,6},{23,7},{24,8},{25... | collective-permute-start | bytes 1352 | tf_op jit(solution)/shard_map/ppermute | solution.py:14
  405.3 5.5 %collective-permute-start.6 = (f32[7,16]{0,1:T(8,128)S(1)}, f32[7,16]{0,1:T(8,128)S(1)}, u32[]{:S(2)}, u32[]{:S(2)}) collective-permute-start(f32[7,16]{0,1:T(8,128)S(1)} %slice.411), channel_id=1, source_target_pairs={{0,16},{1,17},{2,18},{3,19},{4,20},{5,21},{6,22},{7,23},{8,24},{9,... | collective-permute-start | bytes 1352 | tf_op jit(solution)/shard_map/ppermute | solution.py:14
  415.3 19.3 %collective-permute-start.7 = (f32[7,16]{0,1:T(8,128)S(1)}, f32[7,16]{0,1:T(8,128)S(1)}, u32[]{:S(2)}, u32[]{:S(2)}) collective-permute-start(f32[7,16]{0,1:T(8,128)S(1)} %bitcast.28), channel_id=1, source_target_pairs={{16,0},{17,1},{18,2},{19,3},{20,4},{21,5},{22,6},{23,7},{24,8},{25... | collective-permute-start | bytes 1352 | tf_op jit(solution)/shard_map/ppermute | solution.py:14
Sparse Core Ops, SparseCore 0:
  11.4 91.6 all-reduce.2
  106.5 54.8 reduce-scatter.1
where the time goes:
time: 494 us; the launch traced here: 492 us
  blocking collectives  274 us (55%)
  waiting for transfers between devices  135 us (27%)
  matrix products  23.1 us (5%)
  between operations  20.9 us (4%)
  other arithmetic  20.4 us (4%)
  starting transfers between devices  14.7 us (3%)
    psum x5, blocking collectives, global_total(): return lax.psum(value, ('day', 'stu'))  208 us
    all_gather x4, blocking collectives, with_gram(): lax.all_gather(values, 'stu', axis=1, tiled=True)  66.5 us
    psum x1, waiting for transfers between devices, summed_gram(): return lax.psum(local_gram, 'stu')  64.2 us
    reduce_scatter x1, waiting for transfers between devices, local(): lax.psum_scatter(local_terms, 'stu', scatter_dimension=1, tiled=True)  57.7 us
    dot_general x4, matrix products, with_gram(): jnp.dot(lax.all_gather(values, 'stu', axis=1, tiled=True), gram_part, pre...  20.8 us
    sub x4, other arithmetic, filter_rows(): out = out - coef[lag - 1] * extended[LAGS - lag:LAGS - lag + count]  17.8 us
    ppermute x8, starting transfers between devices, shifted(): return lax.ppermute(block, axis, route)  14.6 us
    ppermute x8, waiting for transfers between devices, shifted(): return lax.ppermute(block, axis, route)  12.7 us
  transfers between devices with their start and end apart: 10, of which 5 were waited for; matrix products, arithmetic and copies ran while one was open for 2% of the time, Pallas kernels for 0%

commit v1 on v0

--- a/solution.py
+++ b/solution.py
@@ -2,6 +2,7 @@
 import jax.numpy as jnp
 from jax import lax
 from jax.sharding import PartitionSpec as P
+from jax.lax import psum
 
 LAGS = 7
 ITERS = 3
@@ -47,7 +48,7 @@
 
 
 def global_total(value):
-    return lax.psum(value, ("day", "stu"))
+    return psum(psum(value, "stu"), "day")
 
 
 def summed_gram(local_gram):

time: 494 us -> 473 us (0.957)
  the two profiles are of different devices: /device:TPU:14 before, /device:TPU:0 now
where the time goes in v1:
time: 473 us; the launch traced here: 471 us
  blocking collectives  261 us (55%)
  waiting for transfers between devices  121 us (26%)
  matrix products  23.3 us (5%)
  starting transfers between devices  21.4 us (5%)
  between operations  20.7 us (4%)
  other arithmetic  20.5 us (4%)
    psum x10, blocking collectives, global_total(): return psum(psum(value, 'stu'), 'day')  184 us
    all_gather x4, blocking collectives, with_gram(): lax.all_gather(values, 'stu', axis=1, tiled=True)  76.7 us
    psum x1, waiting for transfers between devices, summed_gram(): return lax.psum(local_gram, 'stu')  58.5 us
    reduce_scatter x1, waiting for transfers between devices, local(): lax.psum_scatter(local_terms, 'stu', scatter_dimension=1, tiled=True)  58.3 us
    ppermute x8, starting transfers between devices, shifted(): return lax.ppermute(block, axis, route)  21.3 us
    dot_general x4, matrix products, with_gram(): jnp.dot(lax.all_gather(values, 'stu', axis=1, tiled=True), gram_part, pre...  20.9 us
    sub x4, other arithmetic, filter_rows(): out = out - coef[lag - 1] * extended[LAGS - lag:LAGS - lag + count]  17.8 us
  transfers between devices with their start and end apart: 10, of which 5 were waited for; matrix products, arithmetic and copies ran while one was open for 2% of the time, Pallas kernels for 0%

profile of v1, /device:TPU:0, one launch (start us, length us, event | category | flops | bytes accessed | tf_op | source)
XLA Modules:
  0.0 471.4 jit_solution(8854464314555483708)
XLA Ops:
  8.3 4.9 %collective-permute-start = (f32[7,16]{0,1:T(8,128)S(1)}, f32[7,16]{0,1:T(8,128)S(1)}, u32[]{:S(2)}, u32[]{:S(2)}) collective-permute-start(f32[7,16]{0,1:T(8,128)S(1)} %slice.333), channel_id=1, source_target_pairs={{0,16},{1,17},{2,18},{3,19},{4,20},{5,21},{6,22},{7,23},{8,24},{9,... | collective-permute-start | bytes 1352 | tf_op jit(solution)/shard_map/ppermute | solution.py:15
  17.9 22.0 %all_gather.12 = f32[32,256]{0,1:T(8,128)S(1)} all-gather(f32[32,16]{0,1:T(8,128)S(1)} %copy.10), channel_id=1, replica_groups=mesh['day'=2,'stu'=16] {'stu'}, dimensions={1}, use_global_device_ids=true | all-gather | bytes 34816 | tf_op jit(solution)/shard_map/all_gather | solution.py:39
  39.9 4.5 fusion.120
  45.7 58.5 %all-reduce.4.cloned.1.call-done = f32[256,256]{0,1:T(8,128)} async-done(((f32[256,256]{0,1:T(8,128)}), f32[256,256]{0,1:T(8,128)}) %all-reduce.4.cloned.1.call-update) | async-done | bytes 262160 | tf_op jit(solution)/shard_map/psum | solution.py:55
  104.9 58.3 %reduce-scatter.2.cloned.1.call-done = f32[32,16]{0,1:T(8,128)} async-done(((f32[32,256]{0,1:T(8,128)}), f32[32,16]{0,1:T(8,128)}) %reduce-scatter.2.cloned.1.call-update) | async-done | bytes 2064 | tf_op jit(solution)/shard_map/reduce_scatter | solution.py:73
  163.2 5.2 %fusion.104 = f32[32,16]{0,1:T(8,128)S(1)} fusion(f32[32,16]{0,1:T(8,128)} %reduce-scatter.2.cloned.1.call-done, f32[7,16]{0,1:T(8,128)S(1)} %collective-permute-done.1, f32[32,16]{0,1:T(8,128)S(1)} %fusion.120, f32[]{:T(128)} %bitcast.7, f32[]{:T(128)} %bitcast.6, f32[]{:T(128)} %bitcast.5, f32[]{:T(128)} %bitcast.4, f32[]{:T(128)} %bitcast.3, ...), kind=kOutput, calls=%fused_computation.173 | convolution fusion | flops 1584640 | bytes 55772 | tf_op jit(solution)/shard_map/dot_general | solution.py:38
  173.2 4.5 fusion.86
  179.0 19.8 %all_gather.13 = f32[32,256]{0,1:T(8,128)S(1)} all-gather(f32[32,16]{0,1:T(8,128)S(1)} %fusion.104), channel_id=1, replica_groups=mesh['day'=2,'stu'=16] {'stu'}, dimensions={1}, use_global_device_ids=true | all-gather | bytes 34816 | tf_op jit(solution)/shard_map/all_gather | solution.py:39
  198.8 5.2 %multiply_reduce_fusion.4 = (f32[]{:T(128)}, f32[]{:T(128)}, f32[32,16]{0,1:T(8,128)S(1)}) fusion(f32[32,16]{0,1:T(8,128)S(1)} %fusion.104, f32[7,16]{0,1:T(8,128)S(1)} %collective-permute-done.3, f32[32,16]{0,1:T(8,128)S(1)} %fusion.86, f32[]{:T(128)} %bitcast.7, f32[]{:T(128)} %bitcast.6, f32[]{:T(128)} %bitcast.5, f32[]{:T(128)} %bitcast.4, ...), kind=kOutput, calls=%fused_computation.235 | convolution fusion | flops 1586174 | bytes 55780 | tf_op jit(solution)/shard_map/dot_general | solution.py:38
  204.0 30.5 %all-reduce = (f32[]{:T(128)}, f32[]{:T(128)}) all-reduce(f32[]{:T(128)} %get-tuple-element.3, f32[]{:T(128)} %get-tuple-element.2), channel_id=1, replica_groups=mesh['day'=2,'stu'=16] {'stu'}, use_global_device_ids=true, to_apply=%region_4.0 | all-reduce | flops 2 | bytes 16 | tf_op jit(solution)/shard_map/psum | solution.py:51
  234.5 6.2 %all-reduce.1 = (f32[]{:T(128)}, f32[]{:T(128)}) all-reduce(f32[]{:T(128)} %get-tuple-element.4, f32[]{:T(128)} %get-tuple-element.5), channel_id=1, replica_groups=mesh['day'=2,'stu'=16] {'day'}, use_global_device_ids=true, to_apply=%region_5.0 | all-reduce | flops 2 | bytes 16 | tf_op jit(solution)/shard_map/psum | solution.py:51
  242.7 30.1 %psum.96 = f32[]{:T(128)} all-reduce(f32[]{:T(128)} %multiply_reduce_fusion.3), channel_id=1, replica_groups=mesh['day'=2,'stu'=16] {'stu'}, use_global_device_ids=true, to_apply=%region_10.0 | all-reduce | flops 1 | bytes 8 | tf_op jit(solution)/shard_map/psum | solution.py:51
  272.9 5.6 %psum.97 = f32[]{:T(128)} all-reduce(f32[]{:T(128)} %psum.96), channel_id=1, replica_groups=mesh['day'=2,'stu'=16] {'day'}, use_global_device_ids=true, to_apply=%region_11.0 | all-reduce | flops 1 | bytes 8 | tf_op jit(solution)/shard_map/psum | solution.py:51
  285.2 4.5 fusion.53
  291.0 17.5 %all_gather.14 = f32[32,256]{0,1:T(8,128)S(1)} all-gather(f32[32,16]{0,1:T(8,128)S(1)} %multiply_add_fusion.2), channel_id=1, replica_groups=mesh['day'=2,'stu'=16] {'stu'}, dimensions={1}, use_global_device_ids=true | all-gather | bytes 34816 | tf_op jit(solution)/shard_map/all_gather | solution.py:39
  308.4 5.2 %multiply_reduce_fusion.2 = (f32[]{:T(128)}, f32[32,16]{0,1:T(8,128)S(1)}) fusion(f32[32,16]{0,1:T(8,128)S(1)} %multiply_add_fusion.2, f32[7,16]{0,1:T(8,128)S(1)} %collective-permute-done.5, f32[32,16]{0,1:T(8,128)S(1)} %fusion.53, f32[]{:T(128)} %bitcast.7, f32[]{:T(128)} %bitcast.6, f32[]{:T(128)} %bitcast.5, f32[]{:T(128)} %bitcast.4, f32[]{:T(128)} %bitcast.3, ...), kind=kOutput, calls=%fused_computation.231 | convolution fusion | flops 1585151 | bytes 55776 | tf_op jit(solution)/shard_map/dot_general | solution.py:38
  313.7 32.0 %psum.98 = f32[]{:T(128)} all-reduce(f32[]{:T(128)} %get-tuple-element.12), channel_id=1, replica_groups=mesh['day'=2,'stu'=16] {'stu'}, use_global_device_ids=true, to_apply=%region_13.0 | all-reduce | flops 1 | bytes 8 | tf_op jit(solution)/shard_map/psum | solution.py:51
  345.7 6.1 %psum.99 = f32[]{:T(128)} all-reduce(f32[]{:T(128)} %psum.98), channel_id=1, replica_groups=mesh['day'=2,'stu'=16] {'day'}, use_global_device_ids=true, to_apply=%region_14.0 | all-reduce | flops 1 | bytes 8 | tf_op jit(solution)/shard_map/psum | solution.py:51
  353.8 30.1 %psum.100 = f32[]{:T(128)} all-reduce(f32[]{:T(128)} %get-tuple-element.10), channel_id=1, replica_groups=mesh['day'=2,'stu'=16] {'stu'}, use_global_device_ids=true, to_apply=%region_16.0 | all-reduce | flops 1 | bytes 8 | tf_op jit(solution)/shard_map/psum | solution.py:51
  383.9 5.6 %psum.101 = f32[]{:T(128)} all-reduce(f32[]{:T(128)} %psum.100), channel_id=1, replica_groups=mesh['day'=2,'stu'=16] {'day'}, use_global_device_ids=true, to_apply=%region_17.0 | all-reduce | flops 1 | bytes 8 | tf_op jit(solution)/shard_map/psum | solution.py:51
  401.8 17.5 %all_gather.15 = f32[32,256]{0,1:T(8,128)S(1)} all-gather(f32[32,16]{0,1:T(8,128)S(1)} %multiply_add_fusion.1), channel_id=1, replica_groups=mesh['day'=2,'stu'=16] {'stu'}, dimensions={1}, use_global_device_ids=true | all-gather | bytes 34816 | tf_op jit(solution)/shard_map/all_gather | solution.py:39
  419.3 5.2 %multiply_reduce_fusion = (f32[]{:T(128)}, f32[32,16]{0,1:T(8,128)S(1)}) fusion(f32[32,16]{0,1:T(8,128)S(1)} %multiply_add_fusion.1, f32[7,16]{0,1:T(8,128)S(1)} %collective-permute-done.7, f32[32,16]{0,1:T(8,128)S(1)} %fusion.20, f32[]{:T(128)} %bitcast.7, f32[]{:T(128)} %bitcast.6, f32[]{:T(128)} %bitcast.5, f32[]{:T(128)} %bitcast.4, f32[]{:T(128)} %bitcast.3, ...), kind=kOutput, calls=%fused_computation.227 | convolution fusion | flops 1585151 | bytes 55776 | tf_op jit(solution)/shard_map/dot_general | solution.py:38
  424.5 32.0 %psum.102 = f32[]{:T(128)} all-reduce(f32[]{:T(128)} %get-tuple-element.8), channel_id=1, replica_groups=mesh['day'=2,'stu'=16] {'stu'}, use_global_device_ids=true, to_apply=%region_19.0 | all-reduce | flops 1 | bytes 8 | tf_op jit(solution)/shard_map/psum | solution.py:51
  456.5 6.1 %psum.103 = f32[]{:T(128)} all-reduce(f32[]{:T(128)} %psum.102), channel_id=1, replica_groups=mesh['day'=2,'stu'=16] {'day'}, use_global_device_ids=true, to_apply=%region_20.0 | all-reduce | flops 1 | bytes 8 | tf_op jit(solution)/shard_map/psum | solution.py:51
  (46 shorter events, 33.6 us)
Async XLA Ops:
  7.2 8.3 %copy-start = (bf16[1024,256]{1,0:T(8,128)(2,1)S(1)}, bf16[1024,256]{1,0:T(8,128)(2,1)}, u32[]{:S(2)}) copy-start(bf16[1024,256]{1,0:T(8,128)(2,1)} %param.7) | copy-start | bytes 1572868
  7.2 8.3 %copy-start.1 = (bf16[32,8,1024]{2,1,0:T(8,128)(2,1)S(1)}, bf16[32,8,1024]{2,1,0:T(8,128)(2,1)}, u32[]{:S(2)}) copy-start(bf16[32,8,1024]{2,1,0:T(8,128)(2,1)} %param.5) | copy-start | bytes 1572868
  7.2 97.0 %all-reduce.4.cloned.1.call-start = ((), (), s32[]{:S(2)}) async-start(), calls=%async_computation.2 | async-start | bytes 524288 | tf_op jit(solution)/shard_map/psum | solution.py:55
  8.3 31.6 %collective-permute-start = (f32[7,16]{0,1:T(8,128)S(1)}, f32[7,16]{0,1:T(8,128)S(1)}, u32[]{:S(2)}, u32[]{:S(2)}) collective-permute-start(f32[7,16]{0,1:T(8,128)S(1)} %slice.333), channel_id=1, source_target_pairs={{0,16},{1,17},{2,18},{3,19},{4,20},{5,21},{6,22},{7,23},{8,24},{9,... | collective-permute-start | bytes 1352 | tf_op jit(solution)/shard_map/ppermute | solution.py:15
  14.8 0.7 copy-start.2
  14.8 148.3 %reduce-scatter.2.cloned.1.call-start = ((), (), s32[]{:S(2)}) async-start(), calls=%async_computation.1 | async-start | bytes 139264 | tf_op jit(solution)/shard_map/reduce_scatter | solution.py:73
  16.6 0.7 copy-start.3
  44.4 60.5 %collective-permute-start.1 = (f32[7,16]{0,1:T(8,128)S(1)}, f32[7,16]{0,1:T(8,128)S(1)}, u32[]{:S(2)}, u32[]{:S(2)}) collective-permute-start(f32[7,16]{0,1:T(8,128)S(1)} %bitcast.27), channel_id=1, source_target_pairs={{16,0},{17,1},{18,2},{19,3},{20,4},{21,5},{22,6},{23,7},{24,8},{25... | collective-permute-start | bytes 1352 | tf_op jit(solution)/shard_map/ppermute | solution.py:15
  168.5 4.7 %collective-permute-start.2 = (f32[7,16]{0,1:T(8,128)S(1)}, f32[7,16]{0,1:T(8,128)S(1)}, u32[]{:S(2)}, u32[]{:S(2)}) collective-permute-start(f32[7,16]{0,1:T(8,128)S(1)} %slice.359), channel_id=1, source_target_pairs={{0,16},{1,17},{2,18},{3,19},{4,20},{5,21},{6,22},{7,23},{8,24},{9,... | collective-permute-start | bytes 1352 | tf_op jit(solution)/shard_map/ppermute | solution.py:15
  177.7 21.1 %collective-permute-start.3 = (f32[7,16]{0,1:T(8,128)S(1)}, f32[7,16]{0,1:T(8,128)S(1)}, u32[]{:S(2)}, u32[]{:S(2)}) collective-permute-start(f32[7,16]{0,1:T(8,128)S(1)} %bitcast.29), channel_id=1, source_target_pairs={{16,0},{17,1},{18,2},{19,3},{20,4},{21,5},{22,6},{23,7},{24,8},{25... | collective-permute-start | bytes 1352 | tf_op jit(solution)/shard_map/ppermute | solution.py:15
  279.9 5.3 %collective-permute-start.4 = (f32[7,16]{0,1:T(8,128)S(1)}, f32[7,16]{0,1:T(8,128)S(1)}, u32[]{:S(2)}, u32[]{:S(2)}) collective-permute-start(f32[7,16]{0,1:T(8,128)S(1)} %slice.385), channel_id=1, source_target_pairs={{0,16},{1,17},{2,18},{3,19},{4,20},{5,21},{6,22},{7,23},{8,24},{9,... | collective-permute-start | bytes 1352 | tf_op jit(solution)/shard_map/ppermute | solution.py:15
  289.7 18.8 %collective-permute-start.5 = (f32[7,16]{0,1:T(8,128)S(1)}, f32[7,16]{0,1:T(8,128)S(1)}, u32[]{:S(2)}, u32[]{:S(2)}) collective-permute-start(f32[7,16]{0,1:T(8,128)S(1)} %bitcast.30), channel_id=1, source_target_pairs={{16,0},{17,1},{18,2},{19,3},{20,4},{21,5},{22,6},{23,7},{24,8},{25... | collective-permute-start | bytes 1352 | tf_op jit(solution)/shard_map/ppermute | solution.py:15
  390.7 5.3 %collective-permute-start.6 = (f32[7,16]{0,1:T(8,128)S(1)}, f32[7,16]{0,1:T(8,128)S(1)}, u32[]{:S(2)}, u32[]{:S(2)}) collective-permute-start(f32[7,16]{0,1:T(8,128)S(1)} %slice.411), channel_id=1, source_target_pairs={{0,16},{1,17},{2,18},{3,19},{4,20},{5,21},{6,22},{7,23},{8,24},{9,... | collective-permute-start | bytes 1352 | tf_op jit(solution)/shard_map/ppermute | solution.py:15
  400.5 18.8 %collective-permute-start.7 = (f32[7,16]{0,1:T(8,128)S(1)}, f32[7,16]{0,1:T(8,128)S(1)}, u32[]{:S(2)}, u32[]{:S(2)}) collective-permute-start(f32[7,16]{0,1:T(8,128)S(1)} %bitcast.28), channel_id=1, source_target_pairs={{16,0},{17,1},{18,2},{19,3},{20,4},{21,5},{22,6},{23,7},{24,8},{25... | collective-permute-start | bytes 1352 | tf_op jit(solution)/shard_map/ppermute | solution.py:15
Sparse Core Ops, SparseCore 0:
  15.0 89.1 all-reduce.3
  107.6 55.5 reduce-scatter.1
